TPU v7x, 512 devices: a whole 4x4x16 slice. The times are simulated.
512 devices in a mesh: ex: 32 (over z, core), pb: 16 (over y, x).
Axes of the slice: x: 4, y: 4, z: 16, core: 2. Of those that a mesh axis runs over, the one named last changes fastest.
Arguments:
- train_sketch: bfloat16 [98304, 8192], P(('ex', 'pb')), may hold values from -6 to 6
- query_sketch: bfloat16 [768, 8192], P('pb'), may hold values from -0.0625 to 0.0625
- residual: float32 [98304], P(('ex', 'pb')), may hold values from 0.05 to 1
- example_source: int32 [98304], P(('ex', 'pb')), may hold values from 0 to 32767, as said below
- source_place: int32 [32768], replicated, may hold values from 0 to 32767, as said below
Outputs:
- source_scores: float32 [32768, 768], P(('ex', 'pb'))
Inputs may be any that keep to these rules, and one draw needn't show every extreme that they name: source_place names each row 0 to 32767 once. `example_source`: of the 192 examples of one device, at most 12 have sources whose table row lies with any one owner (row // 1024); one owner receives exactly 12 from every device. Of them, at most 1 have table rows in any one share of that owner (row % 1024 // (1024 / 16)); in every draw some share of one owner receives exactly 1 from every device.
All inputs are finite; a program needn't handle non-finite values.
Results may differ from a plain program's by a relative error of at most 0.0029.
Values may be sent and summed in bfloat16 or wider, within the bound.
A program may use at most 64 MiB of HBM per device.

v0:
```python
import jax
import jax.numpy as jnp
from jax import lax
from jax.sharding import PartitionSpec as P

SRC_DEV = 1024


def passed_along(value, axis, steps):
    count = lax.axis_size(axis)
    pairs = [(source, (source + steps) % count) for source in range(count)]
    return lax.ppermute(value, axis, pairs)


def on_device(train_sketch, query_sketch, residual, example_source, source_place):
    rows_here = train_sketch.shape[0]
    block_width = query_sketch.shape[0]
    cycle_size = lax.axis_size("pb")
    cycle_index = lax.axis_index("pb")
    queries_all = block_width * cycle_size

    def block_scores(held):
        return jnp.einsum("rk,qk->rq", train_sketch, held, preferred_element_type=jnp.float32)

    initial = jnp.zeros((rows_here, queries_all), jnp.float32)
    initial = lax.dynamic_update_slice_in_dim(
        initial, block_scores(query_sketch), cycle_index * block_width, 1
    )

    def advance(turn_no, state_pair):
        held, table = state_pair
        held = passed_along(held, "pb", 1)
        anchor = (cycle_index - turn_no) % cycle_size
        table = lax.dynamic_update_slice_in_dim(table, block_scores(held), anchor * block_width, 1)
        return (held, table)

    scores = lax.fori_loop(1, cycle_size, advance, (query_sketch, initial))[1]
    weighted = (scores * residual[:, None]).astype(jnp.bfloat16)
    placed = jnp.take(source_place, example_source)
    owner_count = lax.axis_size("ex")
    capacity = max(2, 2 * rows_here // owner_count)
    owner_id = placed // SRC_DEV
    slot_id = placed % SRC_DEV
    onehot_own = (owner_id[:, None] == jnp.arange(owner_count, dtype=jnp.int32)[None, :]).astype(
        jnp.int32
    )
    earlier = jnp.cumsum(onehot_own, axis=0) - onehot_own
    rank_in = jnp.sum(earlier * onehot_own, axis=1)
    target = owner_id * capacity + rank_in
    buffer_rows = (
        jnp.zeros((owner_count * capacity, queries_all), jnp.bfloat16).at[target].set(weighted)
    )
    buffer_slots = jnp.full((owner_count * capacity,), -1, jnp.int32).at[target].set(slot_id)
    got_rows, got_slots = (
        lax.all_to_all(buffer_rows, "ex", split_axis=0, concat_axis=0, tiled=True),
        lax.all_to_all(buffer_slots, "ex", split_axis=0, concat_axis=0, tiled=True),
    )
    onehot = (jnp.arange(SRC_DEV, dtype=jnp.int32)[:, None] == got_slots[None, :]).astype(
        jnp.bfloat16
    )
    partial_table = jnp.dot(onehot, got_rows, preferred_element_type=jnp.float32)
    return lax.psum_scatter(partial_table, "pb", scatter_dimension=0, tiled=True)


def solution(mesh):
    return jax.shard_map(
        on_device,
        mesh=mesh,
        in_specs=(P(("ex", "pb"), None), P("pb", None), P(("ex", "pb")), P(("ex", "pb")), P()),
        out_specs=P(("ex", "pb"), None),
        check_vma=False,
    )
```

profile of v0, /device:TPU:1, one launch (start us, length us, event | category | flops | bytes accessed | tf_op | source)
XLA Modules:
  0.0 557.5 jit_solution(8683815440568300974)
XLA Ops:
  6.5 2.2 copy.29
  14.5 16.7 %all-to-all-start = ((s32[32,12,1]{1,2,0:T(1,128)}), s32[32,12,1]{1,2,0:T(1,128)S(1)}, u32[]{:S(2)}, u32[]{:S(2)}) async-start(s32[32,12,1]{1,2,0:T(1,128)} %bitcast.1), calls=%async_computation | async-start | bytes 32768 | tf_op jit(solution)/shard_map/all_to_all | solution.py:56
  31.3 2.2 convolution_dynamic-update-slice_fusion.1
  34.5 363.2 %while.17 = (s32[]{:T(128)}, bf16[48,8192]{1,0:T(8,128)(2,1)}, f32[192,768]{0,1:T(8,128)}, bf16[192,8192]{1,0:T(8,128)(2,1)S(1)}, s32[]{:T(128)}, /*index=5*/s32...) while((s32[]{:T(128)}, bf16[48,8192]{1,0:T(8,128)(2,1)}, ...), condition=%wide.region_5.6_spmd, body=%wide.region_4.5_spmd.sunk | while | flops 150994960 | bytes 8700224 | solution.py:37
  34.5 3.2 collective-permute-start
  37.8 21.5 %collective-permute-done = bf16[48,8192]{1,0:T(8,128)(2,1)} collective-permute-done((bf16[48,8192]{1,0:T(8,128)(2,1)}, bf16[48,8192]{1,0:T(8,128)(2,1)}, u32[]{:S(2)}, u32[]{:S(2)}) %collective-permute-start) | collective-permute-done | bytes 786464 | tf_op jit(solution)/shard_map/while/body/eval_jaxpr/ppermute | solution.py:12
  59.3 2.1 copy.26
  61.4 2.9 convolution_dynamic-update-slice_fusion.3
  66.2 21.7 %collective-permute-done = bf16[48,8192]{1,0:T(8,128)(2,1)} collective-permute-done((bf16[48,8192]{1,0:T(8,128)(2,1)}, bf16[48,8192]{1,0:T(8,128)(2,1)}, u32[]{:S(2)}, u32[]{:S(2)}) %collective-permute-start) | collective-permute-done | bytes 786464 | tf_op jit(solution)/shard_map/while/body/eval_jaxpr/ppermute | solution.py:12
  87.9 2.1 copy.26
  90.0 2.9 convolution_dynamic-update-slice_fusion.3
  94.8 20.9 %collective-permute-done = bf16[48,8192]{1,0:T(8,128)(2,1)} collective-permute-done((bf16[48,8192]{1,0:T(8,128)(2,1)}, bf16[48,8192]{1,0:T(8,128)(2,1)}, u32[]{:S(2)}, u32[]{:S(2)}) %collective-permute-start) | collective-permute-done | bytes 786464 | tf_op jit(solution)/shard_map/while/body/eval_jaxpr/ppermute | solution.py:12
  115.7 2.1 copy.26
  117.8 2.9 convolution_dynamic-update-slice_fusion.3
  122.6 20.0 %collective-permute-done = bf16[48,8192]{1,0:T(8,128)(2,1)} collective-permute-done((bf16[48,8192]{1,0:T(8,128)(2,1)}, bf16[48,8192]{1,0:T(8,128)(2,1)}, u32[]{:S(2)}, u32[]{:S(2)}) %collective-permute-start) | collective-permute-done | bytes 786464 | tf_op jit(solution)/shard_map/while/body/eval_jaxpr/ppermute | solution.py:12
  142.6 2.1 copy.26
  144.7 2.9 convolution_dynamic-update-slice_fusion.3
  149.5 19.2 %collective-permute-done = bf16[48,8192]{1,0:T(8,128)(2,1)} collective-permute-done((bf16[48,8192]{1,0:T(8,128)(2,1)}, bf16[48,8192]{1,0:T(8,128)(2,1)}, u32[]{:S(2)}, u32[]{:S(2)}) %collective-permute-start) | collective-permute-done | bytes 786464 | tf_op jit(solution)/shard_map/while/body/eval_jaxpr/ppermute | solution.py:12
  168.7 2.1 copy.26
  170.8 2.9 convolution_dynamic-update-slice_fusion.3
  175.6 18.3 %collective-permute-done = bf16[48,8192]{1,0:T(8,128)(2,1)} collective-permute-done((bf16[48,8192]{1,0:T(8,128)(2,1)}, bf16[48,8192]{1,0:T(8,128)(2,1)}, u32[]{:S(2)}, u32[]{:S(2)}) %collective-permute-start) | collective-permute-done | bytes 786464 | tf_op jit(solution)/shard_map/while/body/eval_jaxpr/ppermute | solution.py:12
  193.9 2.1 copy.26
  196.0 2.9 convolution_dynamic-update-slice_fusion.3
  200.8 17.5 %collective-permute-done = bf16[48,8192]{1,0:T(8,128)(2,1)} collective-permute-done((bf16[48,8192]{1,0:T(8,128)(2,1)}, bf16[48,8192]{1,0:T(8,128)(2,1)}, u32[]{:S(2)}, u32[]{:S(2)}) %collective-permute-start) | collective-permute-done | bytes 786464 | tf_op jit(solution)/shard_map/while/body/eval_jaxpr/ppermute | solution.py:12
  218.2 2.1 copy.26
  220.3 2.9 convolution_dynamic-update-slice_fusion.3
  225.1 16.6 %collective-permute-done = bf16[48,8192]{1,0:T(8,128)(2,1)} collective-permute-done((bf16[48,8192]{1,0:T(8,128)(2,1)}, bf16[48,8192]{1,0:T(8,128)(2,1)}, u32[]{:S(2)}, u32[]{:S(2)}) %collective-permute-start) | collective-permute-done | bytes 786464 | tf_op jit(solution)/shard_map/while/body/eval_jaxpr/ppermute | solution.py:12
  241.7 2.1 copy.26
  243.8 2.9 convolution_dynamic-update-slice_fusion.3
  248.6 15.7 %collective-permute-done = bf16[48,8192]{1,0:T(8,128)(2,1)} collective-permute-done((bf16[48,8192]{1,0:T(8,128)(2,1)}, bf16[48,8192]{1,0:T(8,128)(2,1)}, u32[]{:S(2)}, u32[]{:S(2)}) %collective-permute-start) | collective-permute-done | bytes 786464 | tf_op jit(solution)/shard_map/while/body/eval_jaxpr/ppermute | solution.py:12
  264.4 2.1 copy.26
  266.5 2.9 convolution_dynamic-update-slice_fusion.3
  271.3 14.9 %collective-permute-done = bf16[48,8192]{1,0:T(8,128)(2,1)} collective-permute-done((bf16[48,8192]{1,0:T(8,128)(2,1)}, bf16[48,8192]{1,0:T(8,128)(2,1)}, u32[]{:S(2)}, u32[]{:S(2)}) %collective-permute-start) | collective-permute-done | bytes 786464 | tf_op jit(solution)/shard_map/while/body/eval_jaxpr/ppermute | solution.py:12
  288.3 2.9 convolution_dynamic-update-slice_fusion.3
  293.1 14.4 %collective-permute-done = bf16[48,8192]{1,0:T(8,128)(2,1)} collective-permute-done((bf16[48,8192]{1,0:T(8,128)(2,1)}, bf16[48,8192]{1,0:T(8,128)(2,1)}, u32[]{:S(2)}, u32[]{:S(2)}) %collective-permute-start) | collective-permute-done | bytes 786464 | tf_op jit(solution)/shard_map/while/body/eval_jaxpr/ppermute | solution.py:12
  309.6 2.9 convolution_dynamic-update-slice_fusion.3
  314.4 14.4 %collective-permute-done = bf16[48,8192]{1,0:T(8,128)(2,1)} collective-permute-done((bf16[48,8192]{1,0:T(8,128)(2,1)}, bf16[48,8192]{1,0:T(8,128)(2,1)}, u32[]{:S(2)}, u32[]{:S(2)}) %collective-permute-start) | collective-permute-done | bytes 786464 | tf_op jit(solution)/shard_map/while/body/eval_jaxpr/ppermute | solution.py:12
  330.9 2.9 convolution_dynamic-update-slice_fusion.3
  335.7 14.4 %collective-permute-done = bf16[48,8192]{1,0:T(8,128)(2,1)} collective-permute-done((bf16[48,8192]{1,0:T(8,128)(2,1)}, bf16[48,8192]{1,0:T(8,128)(2,1)}, u32[]{:S(2)}, u32[]{:S(2)}) %collective-permute-start) | collective-permute-done | bytes 786464 | tf_op jit(solution)/shard_map/while/body/eval_jaxpr/ppermute | solution.py:12
  352.2 2.9 convolution_dynamic-update-slice_fusion.3
  357.0 14.4 %collective-permute-done = bf16[48,8192]{1,0:T(8,128)(2,1)} collective-permute-done((bf16[48,8192]{1,0:T(8,128)(2,1)}, bf16[48,8192]{1,0:T(8,128)(2,1)}, u32[]{:S(2)}, u32[]{:S(2)}) %collective-permute-start) | collective-permute-done | bytes 786464 | tf_op jit(solution)/shard_map/while/body/eval_jaxpr/ppermute | solution.py:12
  373.5 2.9 convolution_dynamic-update-slice_fusion.3
  378.3 14.4 %collective-permute-done = bf16[48,8192]{1,0:T(8,128)(2,1)} collective-permute-done((bf16[48,8192]{1,0:T(8,128)(2,1)}, bf16[48,8192]{1,0:T(8,128)(2,1)}, u32[]{:S(2)}, u32[]{:S(2)}) %collective-permute-start) | collective-permute-done | bytes 786464 | tf_op jit(solution)/shard_map/while/body/eval_jaxpr/ppermute | solution.py:12
  394.8 2.9 convolution_dynamic-update-slice_fusion.3
  401.6 24.7 %all-to-all-start.1 = ((bf16[32,12,768]{2,1,0:T(8,128)(2,1)}), bf16[32,12,768]{2,1,0:T(8,128)(2,1)S(1)}, u32[]{:S(2)}, u32[]{:S(2)}) async-start(bf16[32,12,768]{2,1,0:T(8,128)(2,1)} %all_to_all.16), calls=%async_computation.1 | async-start | bytes 1572864 | tf_op jit(solution)/shard_map/all_to_all | solution.py:55
  427.7 43.3 %all-to-all-done.1 = bf16[32,12,768]{2,1,0:T(8,128)(2,1)S(1)} async-done(((bf16[32,12,768]{2,1,0:T(8,128)(2,1)}), bf16[32,12,768]{2,1,0:T(8,128)(2,1)S(1)}, u32[]{:S(2)}, u32[]{:S(2)}) %all-to-all-start.1) | async-done | bytes 589856 | tf_op jit(solution)/shard_map/all_to_all | solution.py:55
  471.1 2.6 fusion
  473.8 76.9 %reduce-scatter.2.cloned.1.call-done = f32[64,768]{1,0:T(8,128)} async-done(((f32[1024,768]{1,0:T(8,128)}), f32[64,768]{1,0:T(8,128)}) %reduce-scatter.2.cloned.1.call-update) | async-done | bytes 196624 | tf_op jit(solution)/shard_map/reduce_scatter | solution.py:62
  (55 shorter events, 51.3 us)
Async XLA Ops:
  6.5 2.9 copy-start
  6.5 24.8 %copy-start.1 = (bf16[192,8192]{1,0:T(8,128)(2,1)S(1)}, bf16[192,8192]{1,0:T(8,128)(2,1)}, u32[]{:S(2)}) copy-start(bf16[192,8192]{1,0:T(8,128)(2,1)} %param.7) | copy-start | bytes 9437188
  14.5 387.1 %all-to-all-start = ((s32[32,12,1]{1,2,0:T(1,128)}), s32[32,12,1]{1,2,0:T(1,128)S(1)}, u32[]{:S(2)}, u32[]{:S(2)}) async-start(s32[32,12,1]{1,2,0:T(1,128)} %bitcast.1), calls=%async_computation | async-start | bytes 32768 | tf_op jit(solution)/shard_map/all_to_all | solution.py:56
  33.6 0.9 copy-start.2
  34.5 363.2 %copy-start.3 = (f32[192]{0:T(256)S(1)}, f32[192]{0:T(256)}, u32[]{:S(2)}) copy-start(f32[192]{0:T(256)} %param.9) | copy-start | bytes 2308
  34.5 24.8 %collective-permute-start = (bf16[48,8192]{1,0:T(8,128)(2,1)}, bf16[48,8192]{1,0:T(8,128)(2,1)}, u32[]{:S(2)}, u32[]{:S(2)}) collective-permute-start(bf16[48,8192]{1,0:T(8,128)(2,1)} %get-tuple-element.194), channel_id=1, source_target_pairs={{0,1},{1,2},{2,3},{3,4},{4,5},{5,6},{6,7},{7,8},{8,9},{9,10},{10,1... | collective-permute-start | bytes 2359304 | tf_op jit(solution)/shard_map/while/body/eval_jaxpr/ppermute | solution.py:12
  64.2 23.7 %collective-permute-start = (bf16[48,8192]{1,0:T(8,128)(2,1)}, bf16[48,8192]{1,0:T(8,128)(2,1)}, u32[]{:S(2)}, u32[]{:S(2)}) collective-permute-start(bf16[48,8192]{1,0:T(8,128)(2,1)} %get-tuple-element.194), channel_id=1, source_target_pairs={{0,1},{1,2},{2,3},{3,4},{4,5},{5,6},{6,7},{7,8},{8,9},{9,10},{10,1... | collective-permute-start | bytes 2359304 | tf_op jit(solution)/shard_map/while/body/eval_jaxpr/ppermute | solution.py:12
  92.9 22.8 %collective-permute-start = (bf16[48,8192]{1,0:T(8,128)(2,1)}, bf16[48,8192]{1,0:T(8,128)(2,1)}, u32[]{:S(2)}, u32[]{:S(2)}) collective-permute-start(bf16[48,8192]{1,0:T(8,128)(2,1)} %get-tuple-element.194), channel_id=1, source_target_pairs={{0,1},{1,2},{2,3},{3,4},{4,5},{5,6},{6,7},{7,8},{8,9},{9,10},{10,1... | collective-permute-start | bytes 2359304 | tf_op jit(solution)/shard_map/while/body/eval_jaxpr/ppermute | solution.py:12
  120.7 22.0 %collective-permute-start = (bf16[48,8192]{1,0:T(8,128)(2,1)}, bf16[48,8192]{1,0:T(8,128)(2,1)}, u32[]{:S(2)}, u32[]{:S(2)}) collective-permute-start(bf16[48,8192]{1,0:T(8,128)(2,1)} %get-tuple-element.194), channel_id=1, source_target_pairs={{0,1},{1,2},{2,3},{3,4},{4,5},{5,6},{6,7},{7,8},{8,9},{9,10},{10,1... | collective-permute-start | bytes 2359304 | tf_op jit(solution)/shard_map/while/body/eval_jaxpr/ppermute | solution.py:12
  147.6 21.1 %collective-permute-start = (bf16[48,8192]{1,0:T(8,128)(2,1)}, bf16[48,8192]{1,0:T(8,128)(2,1)}, u32[]{:S(2)}, u32[]{:S(2)}) collective-permute-start(bf16[48,8192]{1,0:T(8,128)(2,1)} %get-tuple-element.194), channel_id=1, source_target_pairs={{0,1},{1,2},{2,3},{3,4},{4,5},{5,6},{6,7},{7,8},{8,9},{9,10},{10,1... | collective-permute-start | bytes 2359304 | tf_op jit(solution)/shard_map/while/body/eval_jaxpr/ppermute | solution.py:12
  173.6 20.3 %collective-permute-start = (bf16[48,8192]{1,0:T(8,128)(2,1)}, bf16[48,8192]{1,0:T(8,128)(2,1)}, u32[]{:S(2)}, u32[]{:S(2)}) collective-permute-start(bf16[48,8192]{1,0:T(8,128)(2,1)} %get-tuple-element.194), channel_id=1, source_target_pairs={{0,1},{1,2},{2,3},{3,4},{4,5},{5,6},{6,7},{7,8},{8,9},{9,10},{10,1... | collective-permute-start | bytes 2359304 | tf_op jit(solution)/shard_map/while/body/eval_jaxpr/ppermute | solution.py:12
  198.8 19.4 %collective-permute-start = (bf16[48,8192]{1,0:T(8,128)(2,1)}, bf16[48,8192]{1,0:T(8,128)(2,1)}, u32[]{:S(2)}, u32[]{:S(2)}) collective-permute-start(bf16[48,8192]{1,0:T(8,128)(2,1)} %get-tuple-element.194), channel_id=1, source_target_pairs={{0,1},{1,2},{2,3},{3,4},{4,5},{5,6},{6,7},{7,8},{8,9},{9,10},{10,1... | collective-permute-start | bytes 2359304 | tf_op jit(solution)/shard_map/while/body/eval_jaxpr/ppermute | solution.py:12
  223.2 18.5 %collective-permute-start = (bf16[48,8192]{1,0:T(8,128)(2,1)}, bf16[48,8192]{1,0:T(8,128)(2,1)}, u32[]{:S(2)}, u32[]{:S(2)}) collective-permute-start(bf16[48,8192]{1,0:T(8,128)(2,1)} %get-tuple-element.194), channel_id=1, source_target_pairs={{0,1},{1,2},{2,3},{3,4},{4,5},{5,6},{6,7},{7,8},{8,9},{9,10},{10,1... | collective-permute-start | bytes 2359304 | tf_op jit(solution)/shard_map/while/body/eval_jaxpr/ppermute | solution.py:12
  246.7 17.7 %collective-permute-start = (bf16[48,8192]{1,0:T(8,128)(2,1)}, bf16[48,8192]{1,0:T(8,128)(2,1)}, u32[]{:S(2)}, u32[]{:S(2)}) collective-permute-start(bf16[48,8192]{1,0:T(8,128)(2,1)} %get-tuple-element.194), channel_id=1, source_target_pairs={{0,1},{1,2},{2,3},{3,4},{4,5},{5,6},{6,7},{7,8},{8,9},{9,10},{10,1... | collective-permute-start | bytes 2359304 | tf_op jit(solution)/shard_map/while/body/eval_jaxpr/ppermute | solution.py:12
  269.3 16.8 %collective-permute-start = (bf16[48,8192]{1,0:T(8,128)(2,1)}, bf16[48,8192]{1,0:T(8,128)(2,1)}, u32[]{:S(2)}, u32[]{:S(2)}) collective-permute-start(bf16[48,8192]{1,0:T(8,128)(2,1)} %get-tuple-element.194), channel_id=1, source_target_pairs={{0,1},{1,2},{2,3},{3,4},{4,5},{5,6},{6,7},{7,8},{8,9},{9,10},{10,1... | collective-permute-start | bytes 2359304 | tf_op jit(solution)/shard_map/while/body/eval_jaxpr/ppermute | solution.py:12
  291.1 16.4 %collective-permute-start = (bf16[48,8192]{1,0:T(8,128)(2,1)}, bf16[48,8192]{1,0:T(8,128)(2,1)}, u32[]{:S(2)}, u32[]{:S(2)}) collective-permute-start(bf16[48,8192]{1,0:T(8,128)(2,1)} %get-tuple-element.194), channel_id=1, source_target_pairs={{0,1},{1,2},{2,3},{3,4},{4,5},{5,6},{6,7},{7,8},{8,9},{9,10},{10,1... | collective-permute-start | bytes 2359304 | tf_op jit(solution)/shard_map/while/body/eval_jaxpr/ppermute | solution.py:12
  312.4 16.4 %collective-permute-start = (bf16[48,8192]{1,0:T(8,128)(2,1)}, bf16[48,8192]{1,0:T(8,128)(2,1)}, u32[]{:S(2)}, u32[]{:S(2)}) collective-permute-start(bf16[48,8192]{1,0:T(8,128)(2,1)} %get-tuple-element.194), channel_id=1, source_target_pairs={{0,1},{1,2},{2,3},{3,4},{4,5},{5,6},{6,7},{7,8},{8,9},{9,10},{10,1... | collective-permute-start | bytes 2359304 | tf_op jit(solution)/shard_map/while/body/eval_jaxpr/ppermute | solution.py:12
  333.7 16.4 %collective-permute-start = (bf16[48,8192]{1,0:T(8,128)(2,1)}, bf16[48,8192]{1,0:T(8,128)(2,1)}, u32[]{:S(2)}, u32[]{:S(2)}) collective-permute-start(bf16[48,8192]{1,0:T(8,128)(2,1)} %get-tuple-element.194), channel_id=1, source_target_pairs={{0,1},{1,2},{2,3},{3,4},{4,5},{5,6},{6,7},{7,8},{8,9},{9,10},{10,1... | collective-permute-start | bytes 2359304 | tf_op jit(solution)/shard_map/while/body/eval_jaxpr/ppermute | solution.py:12
  355.0 16.4 %collective-permute-start = (bf16[48,8192]{1,0:T(8,128)(2,1)}, bf16[48,8192]{1,0:T(8,128)(2,1)}, u32[]{:S(2)}, u32[]{:S(2)}) collective-permute-start(bf16[48,8192]{1,0:T(8,128)(2,1)} %get-tuple-element.194), channel_id=1, source_target_pairs={{0,1},{1,2},{2,3},{3,4},{4,5},{5,6},{6,7},{7,8},{8,9},{9,10},{10,1... | collective-permute-start | bytes 2359304 | tf_op jit(solution)/shard_map/while/body/eval_jaxpr/ppermute | solution.py:12
  376.3 16.4 %collective-permute-start = (bf16[48,8192]{1,0:T(8,128)(2,1)}, bf16[48,8192]{1,0:T(8,128)(2,1)}, u32[]{:S(2)}, u32[]{:S(2)}) collective-permute-start(bf16[48,8192]{1,0:T(8,128)(2,1)} %get-tuple-element.194), channel_id=1, source_target_pairs={{0,1},{1,2},{2,3},{3,4},{4,5},{5,6},{6,7},{7,8},{8,9},{9,10},{10,1... | collective-permute-start | bytes 2359304 | tf_op jit(solution)/shard_map/while/body/eval_jaxpr/ppermute | solution.py:12
  401.6 69.4 %all-to-all-start.1 = ((bf16[32,12,768]{2,1,0:T(8,128)(2,1)}), bf16[32,12,768]{2,1,0:T(8,128)(2,1)S(1)}, u32[]{:S(2)}, u32[]{:S(2)}) async-start(bf16[32,12,768]{2,1,0:T(8,128)(2,1)} %all_to_all.16), calls=%async_computation.1 | async-start | bytes 1572864 | tf_op jit(solution)/shard_map/all_to_all | solution.py:55
  426.3 124.3 %reduce-scatter.2.cloned.1.call-start = ((), (), s32[]{:S(2)}) async-start(), calls=%async_computation.3 | async-start | bytes 3342336 | tf_op jit(solution)/shard_map/reduce_scatter | solution.py:62
Sparse Core Ops, SparseCore 0:
  473.9 76.7 reduce-scatter.1
where the time goes:
time: 560 us; the launch traced here: 558 us
  waiting for transfers between devices  379 us (68%)
  starting transfers between devices  71.5 us (13%)
  matrix products  47.8 us (9%)
  local copies, waits for them, and re-layouts  41.5 us (7%)
  between operations  13.5 us (2%)
    ppermute x15, waiting for transfers between devices, passed_along(): return lax.ppermute(value, axis, pairs)  258 us
    reduce_scatter x1, waiting for transfers between devices, on_device(): lax.psum_scatter(partial_table, 'pb', scatter_dimension=0, tiled=True)  76.9 us
    dot_general x16, matrix products, block_scores(): jnp.einsum('rk,qk->rq', train_sketch, held, preferred_element_type=jnp.fl...  45.1 us
    all_to_all x1, waiting for transfers between devices, on_device(): lax.all_to_all(buffer_rows, 'ex', split_axis=0, concat_axis=0, tiled=True)  43.3 us
    while x15, local copies, waits for them, and re-layouts  31.3 us
    ppermute x15, starting transfers between devices, passed_along(): return lax.ppermute(value, axis, pairs)  30 us
    all_to_all x1, starting transfers between devices, on_device(): lax.all_to_all(buffer_rows, 'ex', split_axis=0, concat_axis=0, tiled=True)  24.7 us
    all_to_all x1, starting transfers between devices, on_device(): lax.all_to_all(buffer_slots, 'ex', split_axis=0, concat_axis=0, tiled=True)  16.7 us
  transfers between devices with their start and end apart: 18, of which 17 were waited for; matrix products, arithmetic and copies ran while one was open for 14% of the time, Pallas kernels for 0%

commit v1 on v0

v1 whole, which is shorter than its diff:
```python
import jax
import jax.numpy as jnp
from jax import lax
from jax.experimental import pallas as pl
from jax.experimental.pallas import tpu as pltpu
from jax.sharding import PartitionSpec as P

MESH = pl.DeviceIdType.MESH
NZ, NC, NY, NX = 16, 2, 4, 4
NPB = NY * NX
ROWS, K = 192, 8192
HALF_K, QUARTER_K = K // 2, K // 4
QROWS, GROUPS, GROW = 24, 3, 8
LANES = NPB * GROW
CAP = 12
ZSLOT = 4 * CAP
PSLOT = 4 * NZ
SHARE = 64
QUERIES = 768
KSTEP = 1024
Z_ORDER = (8, 7, 9, 6, 10, 5, 11, 4, 12, 3, 13, 2, 14, 1, 15)
P_ORDER = (
    (2, 2), (1, 2), (2, 1), (3, 2), (2, 3), (1, 1), (3, 3), (1, 3), (3, 1),
    (0, 2), (2, 0), (0, 1), (1, 0), (0, 3), (3, 0),
)
F32, BF16, I32 = jnp.float32, jnp.bfloat16, jnp.int32
EV_B, EV_C, EV_D, EV_E, EV_F, EV_G = range(6)


def iota(shape, dim):
    return lax.broadcasted_iota(I32, shape, dim)


def mm(a, b, dims=((1,), (0,))):
    return lax.dot_general(a, b, (dims, ((), ())), preferred_element_type=F32)


def onehot(mask):
    return jnp.where(mask, 1.0, 0.0).astype(BF16)


def kernel(
    train, query, res, src, place, out,
    q_all, a_all, tbl, bundle, p1, rescol, score, zs, zr, p2, pe, pr, smat, accb, resb,
    local_sem, ag_recv, ag_send, z_recv, z_send, p_recv, p_send, d_recv, d_send,
):
    ex, pb = lax.axis_index("ex"), lax.axis_index("pb")
    z, c, y, x = ex // NC, ex % NC, pb // NX, pb % NX

    def dev(dz=0, dc=0, dy=0, dx=0):
        return (
            ((z + dz) % NZ) * NC + (c + dc) % NC,
            ((y + dy) % NY) * NX + (x + dx) % NX,
        )

    copy_tbl = pltpu.make_async_copy(place, tbl, local_sem.at[0])
    copy_q = [
        pltpu.make_async_copy(
            query.at[pl.ds(pl.multiple_of(c * QROWS + g * GROW, 8), GROW)],
            q_all.at[g, pb],
            local_sem.at[1 + g],
        )
        for g in range(GROUPS)
    ]
    copy_a = pltpu.make_async_copy(train, a_all.at[c], local_sem.at[4])
    copy_tbl.start()
    for cp in copy_q:
        cp.start()
    copy_a.start()

    barrier = pltpu.get_barrier_semaphore()
    greeted = (
        [dev(dc=1)]
        + [dev(dz=d) for d in range(1, NZ)]
        + [dev(dy=d // NX, dx=d % NX) for d in range(1, NPB)]
    )
    for there in greeted:
        pl.semaphore_signal(barrier, inc=1, device_id=there, device_id_type=MESH)

    copy_tbl.wait()
    ids = src[...]
    table = tbl[...]
    chosen = onehot(iota((256, ROWS), 0) == (ids >> 7))
    high = mm((table >> 7).astype(F32).astype(BF16), chosen, ((0,), (0,)))
    low = mm((table & 127).astype(F32).astype(BF16), chosen, ((0,), (0,)))
    lane = iota((128, ROWS), 0) == (ids & 127)
    placed = jnp.sum(jnp.where(lane, high * 128.0 + low, 0.0), axis=0, keepdims=True)
    placed = placed.astype(I32)
    owner, share, row = placed >> 10, (placed >> 6) & 15, placed & 63
    same = iota((32, ROWS), 0) == owner
    before = onehot(iota((ROWS, ROWS), 0) < iota((ROWS, ROWS), 1))
    rank = jnp.sum(jnp.where(same, mm(onehot(same), before), 0.0), axis=0, keepdims=True)
    core_of = owner & 1
    slot = ((owner >> 1) * ZSLOT + core_of * (2 * CAP) + c * CAP).astype(F32) + rank
    code = (share * 8 + (z % 2) * 4 + c * 2 + core_of + 1).astype(F32)
    row_code = (core_of * SHARE + row + 1).astype(F32)
    line = iota((8, ROWS), 0)
    packed = jnp.where(line == 0, slot, jnp.where(line == 1, code, row_code))
    bundle[c, :, 0:ROWS] = jnp.where(line == 3, res[...], packed)

    for cp in copy_q:
        cp.wait()
    pl.semaphore_wait(barrier, len(greeted))

    def remote(src_ref, dst_ref, send, recv, there):
        cp = pltpu.make_async_remote_copy(
            src_ref=src_ref, dst_ref=dst_ref, send_sem=send, recv_sem=recv,
            device_id=there, device_id_type=MESH,
        )
        cp.start()
        return cp

    pair_bundle = remote(bundle.at[c], bundle.at[c], d_send.at[0], d_recv.at[0], dev(dc=1))

    def source(path, df, ds):
        dy, dx = (ds, df) if path == 0 else (df, ds)
        return ((y + dy) % NY) * NX + (x + dx) % NX

    def pass_on(g, path, df, ds, part, first_axis, step, event):
        along_x = first_axis == (path == 0)
        there = dev(dx=step) if along_x else dev(dy=step)
        start, size = path * HALF_K, HALF_K
        if part is not None:
            start, size = start + part * QUARTER_K, QUARTER_K
        ref = q_all.at[g, source(path, df, ds), :, pl.ds(start, size)]
        remote(ref, ref, ag_send.at[g, path], ag_recv.at[g, path, event], there)

    def arrive(g, path, event, count):
        ref = q_all.at[g, pl.ds(0, count), :, pl.ds(0, HALF_K)]
        pltpu.make_async_copy(ref, ref, ag_recv.at[g, path, event]).wait()

    def both_ways(g, path, df, first_axis, event):
        for step in (1, -1):
            pass_on(g, path, df, 0, None, first_axis, step, event)

    def relay_second(g, path, df):
        pass_on(g, path, df, -1, 0, False, 1, EV_G)
        pass_on(g, path, df, 1, 1, False, -1, EV_G)

    def step_a(g):
        for path in (0, 1):
            both_ways(g, path, 0, True, EV_B)
        for path in (0, 1):
            both_ways(g, path, 0, False, EV_C)

    def step_b(g):
        for path in (0, 1):
            arrive(g, path, EV_B, 2)
            pass_on(g, path, -1, 0, 0, True, 1, EV_D)
            pass_on(g, path, 1, 0, 1, True, -1, EV_D)
            both_ways(g, path, -1, False, EV_E)
            both_ways(g, path, 1, False, EV_E)

    def step_c(g):
        for path in (0, 1):
            arrive(g, path, EV_C, 2)
            relay_second(g, path, 0)

    def step_d(g):
        for path in (0, 1):
            arrive(g, path, EV_D, 1)
            both_ways(g, path, 2, False, EV_F)

    def step_e(g):
        for path in (0, 1):
            arrive(g, path, EV_E, 4)
            relay_second(g, path, -1)
            relay_second(g, path, 1)

    def step_f(g):
        for path in (0, 1):
            arrive(g, path, EV_F, 2)
            relay_second(g, path, 2)

    def step_g(g):
        for path in (0, 1):
            arrive(g, path, EV_G, 4)

    def pack(t, part0, part1):
        rows = mm(p1[0], part0) + mm(p1[1], part1)
        zs[t] = rows.astype(BF16).reshape(NZ, ZSLOT, LANES)
        for d in Z_ORDER:
            remote(zs.at[t, (z + d) % NZ], zr.at[t, z], z_send.at[t], z_recv.at[t], dev(dz=d))
        zr[t, z] = zs[t, z]

    def z_arrive(t):
        ref = zr.at[t, pl.ds(0, NZ - 1)]
        pltpu.make_async_copy(ref, ref, z_recv.at[t]).wait()

    def spread(t):
        for pair in range(NZ // 2):
            rows = zr[t, 2 * pair : 2 * pair + 2].reshape(2 * ZSLOT, LANES)
            got = mm(p2[pair], rows).astype(BF16).reshape(NPB, 8, LANES)
            pe[t, :, 8 * pair : 8 * pair + 8, :] = got
        for dy, dx in P_ORDER:
            there = ((y + dy) % NY) * NX + (x + dx) % NX
            remote(pe.at[t, there], pr.at[t, pb], p_send.at[t], p_recv.at[t], dev(dy=dy, dx=dx))
        pr[t, pb] = pe[t, pb]

    def p_arrive(t):
        ref = pr.at[t, pl.ds(0, NPB - 1)]
        pltpu.make_async_copy(ref, ref, p_recv.at[t]).wait()

    def multiply(g):
        score[...] = jnp.zeros_like(score)

        def some(i, carry):
            k = pl.ds(pl.multiple_of(i * KSTEP, KSTEP), KSTEP)
            held = q_all[g, :, :, k].reshape(LANES, KSTEP)
            for s in (0, 1):
                score[s] += mm(a_all[s, :, k], held, ((1,), (1,)))
            return carry

        lax.fori_loop(0, K // KSTEP, some, 0)
        pack(g + 1, *[(score[s] * rescol[s]).astype(BF16) for s in (0, 1)])

    def finish(g):
        t = g + 1
        p_arrive(t)
        accb[g] = mm(smat[...], pr[t].reshape(NPB * PSLOT, LANES)).reshape(2, SHARE, LANES)
        return remote(accb.at[g, 1 - c], resb.at[g], d_send.at[2 + g], d_recv.at[2 + g], dev(dc=1))

    def place_columns(g, value, half):
        r, col = iota((LANES, QUERIES), 0), iota((LANES, QUERIES), 1)
        move = onehot(col == (r // 8) * 48 + r % 8 + g * GROW + half * QROWS)
        top = value.astype(BF16)
        rest = (value - top.astype(F32)).astype(BF16)
        return mm(top, move) + mm(rest, move)

    step_a(0)
    pair_a = remote(train, a_all.at[c], d_send.at[1], d_recv.at[1], dev(dc=1))
    step_b(0)
    pair_bundle.wait()
    eye = iota((ROWS, ROWS), 0) == iota((ROWS, ROWS), 1)

    def column(s, which):
        picked = jnp.where(eye, bundle[s, which : which + 1, 0:ROWS], 0.0)
        return jnp.sum(picked, axis=1, keepdims=True)

    notes = []
    for s in (0, 1):
        p1[s] = onehot(iota((NZ * ZSLOT, ROWS), 0) == bundle[s, 0:1, 0:ROWS].astype(I32))
        rescol[s] = jnp.broadcast_to(column(s, 3), (ROWS, LANES))
        left = iota((ROWS, LANES), 1) < 64
        notes.append(jnp.where(left, column(s, 1), column(s, 2)).astype(BF16))
    pack(0, *notes)
    step_c(0)
    step_d(0)
    step_a(1)
    step_e(0)
    step_b(1)
    step_f(0)
    step_c(1)
    step_d(1)
    z_arrive(0)
    for pair in range(NZ // 2):
        got = zr[0, 2 * pair : 2 * pair + 2].reshape(2 * ZSLOT, LANES).astype(F32)
        hit = (got[:, 0:1] - 1.0).astype(I32) == iota((2 * ZSLOT, 128), 1)
        p2[pair] = jnp.where(hit, 1.0, 0.0).T.astype(BF16)
    spread(0)
    step_g(0)
    copy_a.wait()
    pair_a.wait()
    multiply(0)
    step_a(2)
    step_e(1)
    step_b(2)
    step_f(1)
    step_c(2)
    step_d(2)
    p_arrive(0)
    got = pr[0].reshape(NPB * PSLOT, LANES).astype(F32)
    hit = (got[:, 64:65] - 1.0).astype(I32) == iota((NPB * PSLOT, 128), 1)
    smat[...] = jnp.where(hit, 1.0, 0.0).T.astype(BF16)
    step_g(1)
    multiply(1)
    z_arrive(1)
    spread(1)
    step_e(2)
    step_f(2)
    step_g(2)
    multiply(2)
    pair_acc = [finish(0)]
    z_arrive(2)
    spread(2)
    pair_acc.append(finish(1))
    total = place_columns(0, accb[0, c], c) + place_columns(1, accb[1, c], c)
    pair_acc[0].wait_recv()
    total += place_columns(0, resb[0], 1 - c)
    pair_acc[1].wait_recv()
    total += place_columns(1, resb[1], 1 - c)
    out[...] = total
    z_arrive(3)
    spread(3)
    pair_acc.append(finish(2))
    total = out[...] + place_columns(2, accb[2, c], c)
    pair_acc[2].wait_recv()
    out[...] = total + place_columns(2, resb[2], 1 - c)

    for cp in pair_acc:
        cp.wait_send()
    for g in range(GROUPS):
        for path in (0, 1):
            ref = q_all.at[g, pl.ds(0, 15), :, pl.ds(0, HALF_K)]
            pltpu.make_async_copy(ref, ref, ag_send.at[g, path]).wait()
    for t in range(GROUPS + 1):
        ref = zs.at[t, pl.ds(0, NZ - 1)]
        pltpu.make_async_copy(ref, ref, z_send.at[t]).wait()
        ref = pe.at[t, pl.ds(0, NPB - 1)]
        pltpu.make_async_copy(ref, ref, p_send.at[t]).wait()


def on_device(train_sketch, query_sketch, residual, example_source, source_place):
    anywhere = pl.BlockSpec(memory_space=pl.ANY)
    local = pl.BlockSpec(memory_space=pltpu.VMEM)
    t = GROUPS + 1
    dma = pltpu.SemaphoreType.DMA
    return pl.pallas_call(
        kernel,
        out_shape=jax.ShapeDtypeStruct((SHARE, QUERIES), F32),
        in_specs=[anywhere, anywhere, local, local, anywhere],
        out_specs=local,
        scratch_shapes=[
            pltpu.VMEM((GROUPS, NPB, GROW, K), BF16),
            pltpu.VMEM((NC, ROWS, K), BF16),
            pltpu.VMEM((256, 128), I32),
            pltpu.VMEM((NC, 8, 256), F32),
            pltpu.VMEM((NC, NZ * ZSLOT, ROWS), BF16),
            pltpu.VMEM((NC, ROWS, LANES), F32),
            pltpu.VMEM((NC, ROWS, LANES), F32),
            pltpu.VMEM((t, NZ, ZSLOT, LANES), BF16),
            pltpu.VMEM((t, NZ, ZSLOT, LANES), BF16),
            pltpu.VMEM((NZ // 2, 128, 2 * ZSLOT), BF16),
            pltpu.VMEM((t, NPB, PSLOT, LANES), BF16),
            pltpu.VMEM((t, NPB, PSLOT, LANES), BF16),
            pltpu.VMEM((128, NPB * PSLOT), BF16),
            pltpu.VMEM((GROUPS, 2, SHARE, LANES), F32),
            pltpu.VMEM((GROUPS, SHARE, LANES), F32),
            dma((5,)),
            dma((GROUPS, 2, 6)),
            dma((GROUPS, 2)),
            dma((t,)),
            dma((t,)),
            dma((t,)),
            dma((t,)),
            dma((2 + GROUPS,)),
            dma((2 + GROUPS,)),
        ],
        compiler_params=pltpu.CompilerParams(
            collective_id=1, has_side_effects=True, vmem_limit_bytes=48 * 1024 * 1024
        ),
        name="scores",
    )(
        train_sketch,
        query_sketch,
        residual.reshape(1, -1),
        example_source.reshape(1, -1),
        source_place.reshape(256, 128),
    )


def solution(mesh):
    return jax.shard_map(
        on_device,
        mesh=mesh,
        in_specs=(P(("ex", "pb"), None), P("pb", None), P(("ex", "pb")), P(("ex", "pb")), P()),
        out_specs=P(("ex", "pb"), None),
        check_vma=False,
    )
```

time: 560 us -> 89.7 us (0.16)
  waiting for transfers between devices: 379 us -> 0 us
  Pallas kernels: 0 us -> 83.5 us
  starting transfers between devices: 71.5 us -> 0 us
  matrix products: 47.8 us -> 0 us
  local copies, waits for them, and re-layouts: 41.5 us -> 5.96 us
  between operations: 13.5 us -> 0.01 us
    ppermute x15 -> x0, waiting for transfers between devices: 258 us -> none  [passed_along(): return lax.ppermute(value, axis, pairs)]
    pallas_call x0 -> x1, Pallas kernels: none -> 83.5 us  [on_device(): pl.pallas_call(kernel, out_shape=jax.ShapeDtypeStruct((SHARE, QUERIES), F...]
    reduce_scatter x1 -> x0, waiting for transfers between devices: 76.9 us -> none  [on_device(): lax.psum_scatter(partial_table, 'pb', scatter_dimension=0, tiled=True)]
    dot_general x17 -> x0, matrix products: 47.8 us -> none  [the longest x16 45.1 us: block_scores(): jnp.einsum('rk,qk->rq', train_sketch, held, preferred_element_type=jnp.fl...]
    all_to_all x2 -> x0, waiting for transfers between devices: 43.3 us -> none  [the longest x1 43.3 us: on_device(): lax.all_to_all(buffer_rows, 'ex', split_axis=0, concat_axis=0, tiled=True)]
    all_to_all x2 -> x0, starting transfers between devices: 41.5 us -> none  [the longest x1 24.7 us: on_device(): lax.all_to_all(buffer_rows, 'ex', split_axis=0, concat_axis=0, tiled=True)]
    while x15 -> x0, local copies, waits for them, and re-layouts: 31.3 us -> none
    ppermute x15 -> x0, starting transfers between devices: 30 us -> none  [passed_along(): return lax.ppermute(value, axis, pairs)]
  transfers between devices with their start and end apart: 18 -> 0, of which waited for: 17 -> 0; matrix products, arithmetic and copies ran while one was open for 14% -> 0% of each run, Pallas kernels for 0% -> 0%
where the time goes in v1:
time: 89.7 us; the launch traced here: 89.5 us
  Pallas kernels  83.5 us (93%)
  local copies, waits for them, and re-layouts  5.96 us (7%)
    pallas_call x1, Pallas kernels, on_device(): pl.pallas_call(kernel, out_shape=jax.ShapeDtypeStruct((SHARE, QUERIES), F...  83.5 us
    unnamed x11, local copies, waits for them, and re-layouts  5.96 us

profile of v1, /device:TPU:1, one launch (start us, length us, event | category | flops | bytes accessed | tf_op | source)
XLA Modules:
  0.0 89.5 jit_solution(6554357307276609372)
XLA Ops:
  0.0 0.0 copy-start
  0.0 1.9 %copy-done = bf16[192,8192]{1,0:T(8,128)(2,1)S(1)} copy-done((bf16[192,8192]{1,0:T(8,128)(2,1)S(1)}, bf16[192,8192]{1,0:T(8,128)(2,1)}, u32[]{:S(2)}) %copy-start) | copy-done | bytes 3145752
  1.9 0.0 copy-start.1
  1.9 1.1 %copy-done.1 = bf16[48,8192]{1,0:T(8,128)(2,1)S(1)} copy-done((bf16[48,8192]{1,0:T(8,128)(2,1)S(1)}, bf16[48,8192]{1,0:T(8,128)(2,1)}, u32[]{:S(2)}) %copy-start.1) | copy-done | bytes 786456
  3.0 0.0 copy-start.2
  3.0 0.9 %copy-done.2 = s32[32768]{0:T(1024)S(1)} copy-done((s32[32768]{0:T(1024)S(1)}, s32[32768]{0:T(1024)}, u32[]{:S(2)}) %copy-start.2) | copy-done | bytes 131096
  3.9 0.0 copy-start.3
  3.9 0.7 copy-done.3
  4.6 0.0 copy-start.4
  4.6 0.7 copy-done.4
  5.3 83.5 %scores.1 = f32[64,768]{1,0:T(8,128)S(1)} custom-call(bf16[192,8192]{1,0:T(8,128)(2,1)S(1)} %copy-done, bf16[48,8192]{1,0:T(8,128)(2,1)S(1)} %copy-done.1, f32[1,192]{1,0:T(1,128)S(1)} %bitcast.4, s32[1,192]{1,0:T(1,128)S(1)} %bitcast.5, s32[256,128]{1,0:T(8,128)S(1)} %bitcast.3), custom_call_target="tpu_custom_call" | custom-call | tf_op jit(solution)/shard_map/scores/pallas_call | solution.py:318
  88.8 0.7 copy.7
Async XLA Ops:
  0.0 1.9 %copy-start = (bf16[192,8192]{1,0:T(8,128)(2,1)S(1)}, bf16[192,8192]{1,0:T(8,128)(2,1)}, u32[]{:S(2)}) copy-start(bf16[192,8192]{1,0:T(8,128)(2,1)} %train.1) | copy-start | bytes 9437188
  1.9 1.1 %copy-start.1 = (bf16[48,8192]{1,0:T(8,128)(2,1)S(1)}, bf16[48,8192]{1,0:T(8,128)(2,1)}, u32[]{:S(2)}) copy-start(bf16[48,8192]{1,0:T(8,128)(2,1)} %query.1) | copy-start | bytes 2359300
  3.0 0.9 %copy-start.2 = (s32[32768]{0:T(1024)S(1)}, s32[32768]{0:T(1024)}, u32[]{:S(2)}) copy-start(s32[32768]{0:T(1024)} %param.9) | copy-start | bytes 393220
  3.9 0.7 copy-start.3
  4.6 0.7 copy-start.4

commit v2 on v1

--- a/solution.py
+++ b/solution.py
@@ -24,7 +24,6 @@
     (0, 2), (2, 0), (0, 1), (1, 0), (0, 3), (3, 0),
 )
 F32, BF16, I32 = jnp.float32, jnp.bfloat16, jnp.int32
-EV_B, EV_C, EV_D, EV_E, EV_F, EV_G = range(6)
 
 
 def iota(shape, dim):
@@ -41,8 +40,9 @@
 
 def kernel(
     train, query, res, src, place, out,
-    q_all, a_all, tbl, bundle, p1, rescol, score, zs, zr, p2, pe, pr, smat, accb, resb,
-    local_sem, ag_recv, ag_send, z_recv, z_send, p_recv, p_send, d_recv, d_send,
+    q_all, a_all, tbl, bundle, p1, rescol, score, zms, zmr, pms, pmr, pmf, zs, zr, p2, pe, pr, smat, accb, resb,
+    z_up, z_down, local_sem, ag_recv, ag_send, zq_recv, zq_send, meta_recv, meta_send,
+    z_recv, z_send, p_recv, p_send, d_recv, d_send,
 ):
     ex, pb = lax.axis_index("ex"), lax.axis_index("pb")
     z, c, y, x = ex // NC, ex % NC, pb // NX, pb % NX
@@ -71,8 +71,9 @@
     barrier = pltpu.get_barrier_semaphore()
     greeted = (
         [dev(dc=1)]
-        + [dev(dz=d) for d in range(1, NZ)]
-        + [dev(dy=d // NX, dx=d % NX) for d in range(1, NPB)]
+        + [dev(dx=d) for d in (1, 2, 3)]
+        + [dev(dy=d) for d in (1, 2, 3)]
+        + [dev(dz=d) for d in (1, NZ - 1)]
     )
     for there in greeted:
         pl.semaphore_signal(barrier, inc=1, device_id=there, device_id_type=MESH)
@@ -91,12 +92,15 @@
     before = onehot(iota((ROWS, ROWS), 0) < iota((ROWS, ROWS), 1))
     rank = jnp.sum(jnp.where(same, mm(onehot(same), before), 0.0), axis=0, keepdims=True)
     core_of = owner & 1
-    slot = ((owner >> 1) * ZSLOT + core_of * (2 * CAP) + c * CAP).astype(F32) + rank
+    spot = (core_of * (2 * CAP) + c * CAP).astype(F32) + rank
+    slot = ((owner >> 1) * ZSLOT).astype(F32) + spot
+    wide = ((owner >> 1) * 128 + (z % 2) * ZSLOT).astype(F32) + spot
     code = (share * 8 + (z % 2) * 4 + c * 2 + core_of + 1).astype(F32)
     row_code = (core_of * SHARE + row + 1).astype(F32)
     line = iota((8, ROWS), 0)
     packed = jnp.where(line == 0, slot, jnp.where(line == 1, code, row_code))
-    bundle[c, :, 0:ROWS] = jnp.where(line == 3, res[...], packed)
+    packed = jnp.where(line == 3, res[...], packed)
+    bundle[c, :, 0:ROWS] = jnp.where(line == 4, wide, packed)
 
     for cp in copy_q:
         cp.wait()
@@ -116,65 +120,59 @@
         dy, dx = (ds, df) if path == 0 else (df, ds)
         return ((y + dy) % NY) * NX + (x + dx) % NX
 
-    def pass_on(g, path, df, ds, part, first_axis, step, event):
-        along_x = first_axis == (path == 0)
-        there = dev(dx=step) if along_x else dev(dy=step)
-        start, size = path * HALF_K, HALF_K
-        if part is not None:
-            start, size = start + part * QUARTER_K, QUARTER_K
-        ref = q_all.at[g, source(path, df, ds), :, pl.ds(start, size)]
-        remote(ref, ref, ag_send.at[g, path], ag_recv.at[g, path, event], there)
+    def columns(g, path):
+        if g > 0:
+            return pl.ds(path * HALF_K, HALF_K)
+        return pl.ds(pl.multiple_of((z % 2) * HALF_K + path * QUARTER_K, 128), QUARTER_K)
+
+    def pass_on(g, path, df, first_axis, event):
+        ref = q_all.at[g, source(path, df, 0), :, columns(g, path)]
+        for step in (2, 1, 3):
+            there = dev(dx=step) if first_axis == (path == 0) else dev(dy=step)
+            remote(ref, ref, ag_send.at[g, path], ag_recv.at[g, path, event], there)
 
     def arrive(g, path, event, count):
-        ref = q_all.at[g, pl.ds(0, count), :, pl.ds(0, HALF_K)]
+        ref = q_all.at[g, pl.ds(0, count), :, pl.ds(0, HALF_K if g > 0 else QUARTER_K)]
         pltpu.make_async_copy(ref, ref, ag_recv.at[g, path, event]).wait()
 
-    def both_ways(g, path, df, first_axis, event):
-        for step in (1, -1):
-            pass_on(g, path, df, 0, None, first_axis, step, event)
-
-    def relay_second(g, path, df):
-        pass_on(g, path, df, -1, 0, False, 1, EV_G)
-        pass_on(g, path, df, 1, 1, False, -1, EV_G)
-
-    def step_a(g):
-        for path in (0, 1):
-            both_ways(g, path, 0, True, EV_B)
-        for path in (0, 1):
-            both_ways(g, path, 0, False, EV_C)
+    def z_share(path, df, ds):
+        ref = q_all.at[0, source(path, df, ds), :, columns(0, path)]
+        remote(ref, ref, zq_send, zq_recv, dev(dz=1 if path == 0 else NZ - 1))
+
+    def z_shared():
+        ref = q_all.at[0, pl.ds(0, NPB - 1), :, pl.ds(0, HALF_K)]
+        pltpu.make_async_copy(ref, ref, zq_recv).wait()
+
+    def step_f(g):
+        for path in (0, 1):
+            pass_on(g, path, 0, True, 0)
+
+    def step_s(g):
+        for path in (0, 1):
+            pass_on(g, path, 0, False, 1)
 
     def step_b(g):
         for path in (0, 1):
-            arrive(g, path, EV_B, 2)
-            pass_on(g, path, -1, 0, 0, True, 1, EV_D)
-            pass_on(g, path, 1, 0, 1, True, -1, EV_D)
-            both_ways(g, path, -1, False, EV_E)
-            both_ways(g, path, 1, False, EV_E)
-
-    def step_c(g):
-        for path in (0, 1):
-            arrive(g, path, EV_C, 2)
-            relay_second(g, path, 0)
-
-    def step_d(g):
-        for path in (0, 1):
-            arrive(g, path, EV_D, 1)
-            both_ways(g, path, 2, False, EV_F)
-
-    def step_e(g):
-        for path in (0, 1):
-            arrive(g, path, EV_E, 4)
-            relay_second(g, path, -1)
-            relay_second(g, path, 1)
-
-    def step_f(g):
-        for path in (0, 1):
-            arrive(g, path, EV_F, 2)
-            relay_second(g, path, 2)
+            arrive(g, path, 0, 3)
+        for df in (2, 1, 3):
+            for path in (0, 1):
+                pass_on(g, path, df, False, 2)
 
     def step_g(g):
         for path in (0, 1):
-            arrive(g, path, EV_G, 4)
+            arrive(g, path, 1, 3)
+            arrive(g, path, 2, 9)
+
+    def z_tell():
+        pl.semaphore_signal(z_up, inc=1, device_id=dev(dz=1), device_id_type=MESH)
+        pl.semaphore_signal(z_down, inc=1, device_id=dev(dz=NZ - 1), device_id_type=MESH)
+
+    def z_hear(rounds):
+        for r in rounds:
+            pl.semaphore_wait(z_up, 1)
+            pl.semaphore_wait(z_down, 1)
+            if r < NZ // 2 - 1:
+                z_tell()
 
     def pack(t, part0, part1):
         rows = mm(p1[0], part0) + mm(p1[1], part1)
@@ -212,12 +210,11 @@
             return carry
 
         lax.fori_loop(0, K // KSTEP, some, 0)
-        pack(g + 1, *[(score[s] * rescol[s]).astype(BF16) for s in (0, 1)])
+        pack(g, *[(score[s] * rescol[s]).astype(BF16) for s in (0, 1)])
 
     def finish(g):
-        t = g + 1
-        p_arrive(t)
-        accb[g] = mm(smat[...], pr[t].reshape(NPB * PSLOT, LANES)).reshape(2, SHARE, LANES)
+        p_arrive(g)
+        accb[g] = mm(smat[...], pr[g].reshape(NPB * PSLOT, LANES)).reshape(2, SHARE, LANES)
         return remote(accb.at[g, 1 - c], resb.at[g], d_send.at[2 + g], d_recv.at[2 + g], dev(dc=1))
 
     def place_columns(g, value, half):
@@ -227,62 +224,96 @@
         rest = (value - top.astype(F32)).astype(BF16)
         return mm(top, move) + mm(rest, move)
 
-    step_a(0)
-    pair_a = remote(train, a_all.at[c], d_send.at[1], d_recv.at[1], dev(dc=1))
-    step_b(0)
-    pair_bundle.wait()
-    eye = iota((ROWS, ROWS), 0) == iota((ROWS, ROWS), 1)
-
-    def column(s, which):
+    def column(which, s):
+        eye = iota((ROWS, ROWS), 0) == iota((ROWS, ROWS), 1)
         picked = jnp.where(eye, bundle[s, which : which + 1, 0:ROWS], 0.0)
         return jnp.sum(picked, axis=1, keepdims=True)
 
-    notes = []
-    for s in (0, 1):
-        p1[s] = onehot(iota((NZ * ZSLOT, ROWS), 0) == bundle[s, 0:1, 0:ROWS].astype(I32))
-        rescol[s] = jnp.broadcast_to(column(s, 3), (ROWS, LANES))
-        left = iota((ROWS, LANES), 1) < 64
-        notes.append(jnp.where(left, column(s, 1), column(s, 2)).astype(BF16))
-    pack(0, *notes)
-    step_c(0)
-    step_d(0)
-    step_a(1)
-    step_e(0)
+    def prepare():
+        notes = jnp.zeros((8, NZ * 128), F32)
+        for s in (0, 1):
+            p1[s] = onehot(iota((NZ * ZSLOT, ROWS), 0) == bundle[s, 0:1, 0:ROWS].astype(I32))
+            rescol[s] = jnp.broadcast_to(column(3, s), (ROWS, LANES))
+            spots = onehot(iota((NZ * 128, ROWS), 0) == bundle[s, 4:5, 0:ROWS].astype(I32))
+            values = jnp.where(iota((8, ROWS), 0) < 3, bundle[s, :, 0:ROWS], 0.0).astype(BF16)
+            notes += mm(values, spots, ((1,), (1,)))
+        for k in range(NZ):
+            zms[k] = notes[:, k * 128 : k * 128 + 128].astype(BF16)
+
+    def meta_z():
+        for d in Z_ORDER:
+            remote(zms.at[(z + d) % NZ], zmr.at[z], meta_send.at[0], meta_recv.at[0], dev(dz=d))
+        zmr[z] = zms[z]
+
+    def meta_plane():
+        ref = zmr.at[pl.ds(0, NZ - 1)]
+        pltpu.make_async_copy(ref, ref, meta_recv.at[0]).wait()
+        for pair in range(NZ // 2):
+            both = zmr[2 * pair].astype(F32) + zmr[2 * pair + 1].astype(F32)
+            both = both[:, 0 : 2 * ZSLOT]
+            p2[pair] = onehot(iota((128, 2 * ZSLOT), 0) == both[1:2].astype(I32) - 1)
+            pmf[pair : pair + 1] = mm(both.astype(BF16), p2[pair], ((1,), (1,)))[2:3]
+        pms[...] = pmf[...].astype(BF16)
+        for dy, dx in P_ORDER:
+            remote(pms, pmr.at[pb], meta_send.at[1], meta_recv.at[1], dev(dy=dy, dx=dx))
+        pmr[pb] = pms[...]
+
+    def meta_sum():
+        ref = pmr.at[pl.ds(0, NPB - 1)]
+        pltpu.make_async_copy(ref, ref, meta_recv.at[1]).wait()
+        told = pmr[...].reshape(NPB * 8, 128)
+        u = iota((NPB * PSLOT, 128), 0)
+        spread_out = mm(onehot(u // 8 == iota((NPB * PSLOT, 128), 1)), told)
+        mine = iota((NPB * PSLOT, 128), 1) == pb * 8 + u % 8
+        value = jnp.sum(jnp.where(mine, spread_out, 0.0), axis=1, keepdims=True)
+        hit = value.astype(I32) - 1 == iota((NPB * PSLOT, 128), 1)
+        smat[...] = jnp.where(hit, 1.0, 0.0).T.astype(BF16)
+
+    z_tell()
+    step_f(0)
+    step_s(0)
+    step_f(1)
+    pair_a = remote(train, a_all.at[c], d_send.at[1], d_recv.at[1], dev(dc=1))
+    pair_bundle.wait()
+    prepare()
+    z_hear(range(0, 3))
+    step_b(0)
+    for df in (1, 2, 3):
+        for path in (0, 1):
+            z_share(path, df, 0)
+    step_s(1)
+    for path in (0, 1):
+        arrive(0, path, 1, 3)
+    for ds in (1, 2, 3):
+        for path in (0, 1):
+            z_share(path, 0, ds)
+    z_hear(range(3, NZ // 2))
+    meta_z()
     step_b(1)
-    step_f(0)
-    step_c(1)
-    step_d(1)
-    z_arrive(0)
-    for pair in range(NZ // 2):
-        got = zr[0, 2 * pair : 2 * pair + 2].reshape(2 * ZSLOT, LANES).astype(F32)
-        hit = (got[:, 0:1] - 1.0).astype(I32) == iota((2 * ZSLOT, 128), 1)
-        p2[pair] = jnp.where(hit, 1.0, 0.0).T.astype(BF16)
-    spread(0)
-    step_g(0)
+    for path in (0, 1):
+        arrive(0, path, 2, 9)
+    for df in (1, 2, 3):
+        for ds in (1, 2, 3):
+            for path in (0, 1):
+                z_share(path, df, ds)
+    step_f(2)
+    step_s(2)
+    meta_plane()
     copy_a.wait()
     pair_a.wait()
+    z_shared()
     multiply(0)
-    step_a(2)
-    step_e(1)
     step_b(2)
-    step_f(1)
-    step_c(2)
-    step_d(2)
-    p_arrive(0)
-    got = pr[0].reshape(NPB * PSLOT, LANES).astype(F32)
-    hit = (got[:, 64:65] - 1.0).astype(I32) == iota((NPB * PSLOT, 128), 1)
-    smat[...] = jnp.where(hit, 1.0, 0.0).T.astype(BF16)
     step_g(1)
     multiply(1)
-    z_arrive(1)
-    spread(1)
-    step_e(2)
-    step_f(2)
+    meta_sum()
+    z_arrive(0)
+    spread(0)
     step_g(2)
     multiply(2)
     pair_acc = [finish(0)]
-    z_arrive(2)
-    spread(2)
+    z_arrive(1)
+    spread(1)
     pair_acc.append(finish(1))
     total = place_columns(0, accb[0, c], c) + place_columns(1, accb[1, c], c)
     pair_acc[0].wait_recv()
@@ -290,8 +321,8 @@
     pair_acc[1].wait_recv()
     total += place_columns(1, resb[1], 1 - c)
     out[...] = total
-    z_arrive(3)
-    spread(3)
+    z_arrive(2)
+    spread(2)
     pair_acc.append(finish(2))
     total = out[...] + place_columns(2, accb[2, c], c)
     pair_acc[2].wait_recv()
@@ -301,19 +332,24 @@
         cp.wait_send()
     for g in range(GROUPS):
         for path in (0, 1):
-            ref = q_all.at[g, pl.ds(0, 15), :, pl.ds(0, HALF_K)]
+            ref = q_all.at[g, pl.ds(0, 15), :, pl.ds(0, HALF_K if g > 0 else QUARTER_K)]
             pltpu.make_async_copy(ref, ref, ag_send.at[g, path]).wait()
-    for t in range(GROUPS + 1):
-        ref = zs.at[t, pl.ds(0, NZ - 1)]
-        pltpu.make_async_copy(ref, ref, z_send.at[t]).wait()
-        ref = pe.at[t, pl.ds(0, NPB - 1)]
-        pltpu.make_async_copy(ref, ref, p_send.at[t]).wait()
+        ref = zs.at[g, pl.ds(0, NZ - 1)]
+        pltpu.make_async_copy(ref, ref, z_send.at[g]).wait()
+        ref = pe.at[g, pl.ds(0, NPB - 1)]
+        pltpu.make_async_copy(ref, ref, p_send.at[g]).wait()
+    ref = q_all.at[0, pl.ds(0, NPB - 1), :, pl.ds(0, HALF_K)]
+    pltpu.make_async_copy(ref, ref, zq_send).wait()
+    ref = zms.at[pl.ds(0, NZ - 1)]
+    pltpu.make_async_copy(ref, ref, meta_send.at[0]).wait()
+    ref = pmr.at[pl.ds(0, NPB - 1)]
+    pltpu.make_async_copy(ref, ref, meta_send.at[1]).wait()
 
 
 def on_device(train_sketch, query_sketch, residual, example_source, source_place):
-    anywhere = pl.BlockSpec(memory_space=pl.ANY)
+    anywhere = pl.BlockSpec(memory_space=pltpu.HBM)
     local = pl.BlockSpec(memory_space=pltpu.VMEM)
-    t = GROUPS + 1
+    t = GROUPS
     dma = pltpu.SemaphoreType.DMA
     return pl.pallas_call(
         kernel,
@@ -328,6 +364,11 @@
             pltpu.VMEM((NC, NZ * ZSLOT, ROWS), BF16),
             pltpu.VMEM((NC, ROWS, LANES), F32),
             pltpu.VMEM((NC, ROWS, LANES), F32),
+            pltpu.VMEM((NZ, 8, 128), BF16),
+            pltpu.VMEM((NZ, 8, 128), BF16),
+            pltpu.VMEM((8, 128), BF16),
+            pltpu.VMEM((NPB, 8, 128), BF16),
+            pltpu.VMEM((8, 128), F32),
             pltpu.VMEM((t, NZ, ZSLOT, LANES), BF16),
             pltpu.VMEM((t, NZ, ZSLOT, LANES), BF16),
             pltpu.VMEM((NZ // 2, 128, 2 * ZSLOT), BF16),
@@ -336,9 +377,15 @@
             pltpu.VMEM((128, NPB * PSLOT), BF16),
             pltpu.VMEM((GROUPS, 2, SHARE, LANES), F32),
             pltpu.VMEM((GROUPS, SHARE, LANES), F32),
+            pltpu.SemaphoreType.REGULAR,
+            pltpu.SemaphoreType.REGULAR,
             dma((5,)),
-            dma((GROUPS, 2, 6)),
+            dma((GROUPS, 2, 3)),
             dma((GROUPS, 2)),
+            dma,
+            dma,
+            dma((2,)),
+            dma((2,)),
             dma((t,)),
             dma((t,)),
             dma((t,)),

time: 89.7 us -> 80.8 us (0.901)
  Pallas kernels: 83.5 us -> 74.6 us
    pallas_call x1, Pallas kernels: 83.5 us -> 74.6 us  [on_device(): pl.pallas_call(kernel, out_shape=jax.ShapeDtypeStruct((SHARE, QUERIES), F...]
where the time goes in v2:
time: 80.8 us; the launch traced here: 80.6 us
  Pallas kernels  74.6 us (92%)
  local copies, waits for them, and re-layouts  5.96 us (7%)
    pallas_call x1, Pallas kernels, on_device(): pl.pallas_call(kernel, out_shape=jax.ShapeDtypeStruct((SHARE, QUERIES), F...  74.6 us
    unnamed x11, local copies, waits for them, and re-layouts  5.96 us

profile of v2, /device:TPU:1, one launch (start us, length us, event | category | flops | bytes accessed | tf_op | source)
XLA Modules:
  0.0 80.6 jit_solution(4387840071754056921)
XLA Ops:
  0.0 0.0 copy-start
  0.0 1.9 %copy-done = bf16[192,8192]{1,0:T(8,128)(2,1)S(1)} copy-done((bf16[192,8192]{1,0:T(8,128)(2,1)S(1)}, bf16[192,8192]{1,0:T(8,128)(2,1)}, u32[]{:S(2)}) %copy-start) | copy-done | bytes 3145752
  1.9 0.0 copy-start.1
  1.9 1.1 %copy-done.1 = bf16[48,8192]{1,0:T(8,128)(2,1)S(1)} copy-done((bf16[48,8192]{1,0:T(8,128)(2,1)S(1)}, bf16[48,8192]{1,0:T(8,128)(2,1)}, u32[]{:S(2)}) %copy-start.1) | copy-done | bytes 786456
  3.0 0.0 copy-start.2
  3.0 0.9 %copy-done.2 = s32[32768]{0:T(1024)S(1)} copy-done((s32[32768]{0:T(1024)S(1)}, s32[32768]{0:T(1024)}, u32[]{:S(2)}) %copy-start.2) | copy-done | bytes 131096
  3.9 0.0 copy-start.3
  3.9 0.7 copy-done.3
  4.6 0.0 copy-start.4
  4.6 0.7 copy-done.4
  5.3 74.6 %scores.1 = f32[64,768]{1,0:T(8,128)S(1)} custom-call(bf16[192,8192]{1,0:T(8,128)(2,1)S(1)} %copy-done, bf16[48,8192]{1,0:T(8,128)(2,1)S(1)} %copy-done.1, f32[1,192]{1,0:T(1,128)S(1)} %bitcast.4, s32[1,192]{1,0:T(1,128)S(1)} %bitcast.5, s32[256,128]{1,0:T(8,128)S(1)} %bitcast.3), custom_call_target="tpu_custom_call" | custom-call | tf_op jit(solution)/shard_map/scores/pallas_call | solution.py:354
  79.9 0.7 copy.7
Async XLA Ops:
  0.0 1.9 %copy-start = (bf16[192,8192]{1,0:T(8,128)(2,1)S(1)}, bf16[192,8192]{1,0:T(8,128)(2,1)}, u32[]{:S(2)}) copy-start(bf16[192,8192]{1,0:T(8,128)(2,1)} %train.1) | copy-start | bytes 9437188
  1.9 1.1 %copy-start.1 = (bf16[48,8192]{1,0:T(8,128)(2,1)S(1)}, bf16[48,8192]{1,0:T(8,128)(2,1)}, u32[]{:S(2)}) copy-start(bf16[48,8192]{1,0:T(8,128)(2,1)} %query.1) | copy-start | bytes 2359300
  3.0 0.9 %copy-start.2 = (s32[32768]{0:T(1024)S(1)}, s32[32768]{0:T(1024)}, u32[]{:S(2)}) copy-start(s32[32768]{0:T(1024)} %param.9) | copy-start | bytes 393220
  3.9 0.7 copy-start.3
  4.6 0.7 copy-start.4

commit v3 on v2

--- a/solution.py
+++ b/solution.py
@@ -18,6 +18,7 @@
 SHARE = 64
 QUERIES = 768
 KSTEP = 1024
+PAIR_ORDER = (4, 3, 5, 2, 6, 1, 7, 0)
 Z_ORDER = (8, 7, 9, 6, 10, 5, 11, 4, 12, 3, 13, 2, 14, 1, 15)
 P_ORDER = (
     (2, 2), (1, 2), (2, 1), (3, 2), (2, 3), (1, 1), (3, 3), (1, 3), (3, 1),
@@ -73,34 +74,10 @@
         [dev(dc=1)]
         + [dev(dx=d) for d in (1, 2, 3)]
         + [dev(dy=d) for d in (1, 2, 3)]
-        + [dev(dz=d) for d in (1, NZ - 1)]
+        + [dev(dz=d) for d in (1, 2, 3, 4, 12, 13, 14, 15)]
     )
     for there in greeted:
         pl.semaphore_signal(barrier, inc=1, device_id=there, device_id_type=MESH)
-
-    copy_tbl.wait()
-    ids = src[...]
-    table = tbl[...]
-    chosen = onehot(iota((256, ROWS), 0) == (ids >> 7))
-    high = mm((table >> 7).astype(F32).astype(BF16), chosen, ((0,), (0,)))
-    low = mm((table & 127).astype(F32).astype(BF16), chosen, ((0,), (0,)))
-    lane = iota((128, ROWS), 0) == (ids & 127)
-    placed = jnp.sum(jnp.where(lane, high * 128.0 + low, 0.0), axis=0, keepdims=True)
-    placed = placed.astype(I32)
-    owner, share, row = placed >> 10, (placed >> 6) & 15, placed & 63
-    same = iota((32, ROWS), 0) == owner
-    before = onehot(iota((ROWS, ROWS), 0) < iota((ROWS, ROWS), 1))
-    rank = jnp.sum(jnp.where(same, mm(onehot(same), before), 0.0), axis=0, keepdims=True)
-    core_of = owner & 1
-    spot = (core_of * (2 * CAP) + c * CAP).astype(F32) + rank
-    slot = ((owner >> 1) * ZSLOT).astype(F32) + spot
-    wide = ((owner >> 1) * 128 + (z % 2) * ZSLOT).astype(F32) + spot
-    code = (share * 8 + (z % 2) * 4 + c * 2 + core_of + 1).astype(F32)
-    row_code = (core_of * SHARE + row + 1).astype(F32)
-    line = iota((8, ROWS), 0)
-    packed = jnp.where(line == 0, slot, jnp.where(line == 1, code, row_code))
-    packed = jnp.where(line == 3, res[...], packed)
-    bundle[c, :, 0:ROWS] = jnp.where(line == 4, wide, packed)
 
     for cp in copy_q:
         cp.wait()
@@ -114,26 +91,56 @@
         cp.start()
         return cp
 
-    pair_bundle = remote(bundle.at[c], bundle.at[c], d_send.at[0], d_recv.at[0], dev(dc=1))
+    def meta_own():
+        copy_tbl.wait()
+        ids = src[...]
+        table = tbl[...]
+        chosen = onehot(iota((256, ROWS), 0) == (ids >> 7))
+        high = mm((table >> 7).astype(F32).astype(BF16), chosen, ((0,), (0,)))
+        low = mm((table & 127).astype(F32).astype(BF16), chosen, ((0,), (0,)))
+        lane = iota((128, ROWS), 0) == (ids & 127)
+        placed = jnp.sum(jnp.where(lane, high * 128.0 + low, 0.0), axis=0, keepdims=True)
+        placed = placed.astype(I32)
+        owner, share, row = placed >> 10, (placed >> 6) & 15, placed & 63
+        same = iota((32, ROWS), 0) == owner
+        before = onehot(iota((ROWS, ROWS), 0) < iota((ROWS, ROWS), 1))
+        rank = jnp.sum(jnp.where(same, mm(onehot(same), before), 0.0), axis=0, keepdims=True)
+        core_of = owner & 1
+        spot = (core_of * (2 * CAP) + c * CAP).astype(F32) + rank
+        slot = ((owner >> 1) * ZSLOT).astype(F32) + spot
+        wide = ((owner >> 1) * 128 + (z % 2) * ZSLOT).astype(F32) + spot
+        code = (share * 8 + (z % 2) * 4 + c * 2 + core_of + 1).astype(F32)
+        row_code = (core_of * SHARE + row + 1).astype(F32)
+        line = iota((8, ROWS), 0)
+        packed = jnp.where(line == 0, slot, jnp.where(line == 1, code, row_code))
+        packed = jnp.where(line == 3, res[...], packed)
+        bundle[c, :, 0:ROWS] = jnp.where(line == 4, wide, packed)
 
     def source(path, df, ds):
         dy, dx = (ds, df) if path == 0 else (df, ds)
         return ((y + dy) % NY) * NX + (x + dx) % NX
 
-    def columns(g, path):
-        if g > 0:
+    def columns(g, path, part=0):
+        if g == 1:
             return pl.ds(path * HALF_K, HALF_K)
-        return pl.ds(pl.multiple_of((z % 2) * HALF_K + path * QUARTER_K, 128), QUARTER_K)
-
-    def pass_on(g, path, df, first_axis, event):
-        ref = q_all.at[g, source(path, df, 0), :, columns(g, path)]
+        start = path * HALF_K + part * QUARTER_K
+        if g == 0:
+            start = pl.multiple_of((z % 2) * HALF_K + path * QUARTER_K, 128)
+        return pl.ds(start, QUARTER_K)
+
+    def parts(g):
+        return (0, 1) if g == 2 else (0,)
+
+    def pass_on(g, path, df, first_axis, event, part=0):
+        ref = q_all.at[g, source(path, df, 0), :, columns(g, path, part)]
         for step in (2, 1, 3):
             there = dev(dx=step) if first_axis == (path == 0) else dev(dy=step)
-            remote(ref, ref, ag_send.at[g, path], ag_recv.at[g, path, event], there)
-
-    def arrive(g, path, event, count):
-        ref = q_all.at[g, pl.ds(0, count), :, pl.ds(0, HALF_K if g > 0 else QUARTER_K)]
-        pltpu.make_async_copy(ref, ref, ag_recv.at[g, path, event]).wait()
+            arrived = ag_recv.at[g, path, event, part]
+            remote(ref, ref, ag_send.at[g, path, part], arrived, there)
+
+    def arrive(g, path, event, count, part=0):
+        ref = q_all.at[g, pl.ds(0, count), :, pl.ds(0, HALF_K if g == 1 else QUARTER_K)]
+        pltpu.make_async_copy(ref, ref, ag_recv.at[g, path, event, part]).wait()
 
     def z_share(path, df, ds):
         ref = q_all.at[0, source(path, df, ds), :, columns(0, path)]
@@ -144,72 +151,89 @@
         pltpu.make_async_copy(ref, ref, zq_recv).wait()
 
     def step_f(g):
+        for part in parts(g):
+            for path in (0, 1):
+                pass_on(g, path, 0, True, 0, part)
+
+    def step_s(g):
+        for part in parts(g):
+            for path in (0, 1):
+                pass_on(g, path, 0, False, 1, part)
+
+    def step_b(g):
+        for part in parts(g):
+            for path in (0, 1):
+                arrive(g, path, 0, 3, part)
+            for df in (2, 1, 3):
+                for path in (0, 1):
+                    pass_on(g, path, df, False, 2, part)
+
+    def step_g(g, part=0):
         for path in (0, 1):
-            pass_on(g, path, 0, True, 0)
-
-    def step_s(g):
-        for path in (0, 1):
-            pass_on(g, path, 0, False, 1)
-
-    def step_b(g):
-        for path in (0, 1):
-            arrive(g, path, 0, 3)
-        for df in (2, 1, 3):
-            for path in (0, 1):
-                pass_on(g, path, df, False, 2)
-
-    def step_g(g):
-        for path in (0, 1):
-            arrive(g, path, 1, 3)
-            arrive(g, path, 2, 9)
+            arrive(g, path, 1, 3, part)
+            arrive(g, path, 2, 9, part)
 
     def z_tell():
-        pl.semaphore_signal(z_up, inc=1, device_id=dev(dz=1), device_id_type=MESH)
-        pl.semaphore_signal(z_down, inc=1, device_id=dev(dz=NZ - 1), device_id_type=MESH)
-
-    def z_hear(rounds):
-        for r in rounds:
-            pl.semaphore_wait(z_up, 1)
-            pl.semaphore_wait(z_down, 1)
-            if r < NZ // 2 - 1:
-                z_tell()
+        pl.semaphore_signal(z_up, inc=1, device_id=dev(dz=4), device_id_type=MESH)
+        pl.semaphore_signal(z_down, inc=1, device_id=dev(dz=NZ - 4), device_id_type=MESH)
+
+    def z_hear():
+        pl.semaphore_wait(z_up, 1)
+        pl.semaphore_wait(z_down, 1)
+
+    def send_z(t):
+        for d in Z_ORDER:
+            half = ((z // 2 - ((z + d) % NZ) // 2 + 14) % 8) // 4
+            remote(
+                zs.at[t, (z + d) % NZ], zr.at[t, z], z_send.at[t], z_recv.at[t, half], dev(dz=d)
+            )
+        zr[t, z] = zs[t, z]
 
     def pack(t, part0, part1):
         rows = mm(p1[0], part0) + mm(p1[1], part1)
         zs[t] = rows.astype(BF16).reshape(NZ, ZSLOT, LANES)
-        for d in Z_ORDER:
-            remote(zs.at[t, (z + d) % NZ], zr.at[t, z], z_send.at[t], z_recv.at[t], dev(dz=d))
-        zr[t, z] = zs[t, z]
-
-    def z_arrive(t):
-        ref = zr.at[t, pl.ds(0, NZ - 1)]
-        pltpu.make_async_copy(ref, ref, z_recv.at[t]).wait()
-
-    def spread(t):
-        for pair in range(NZ // 2):
-            rows = zr[t, 2 * pair : 2 * pair + 2].reshape(2 * ZSLOT, LANES)
-            got = mm(p2[pair], rows).astype(BF16).reshape(NPB, 8, LANES)
-            pe[t, :, 8 * pair : 8 * pair + 8, :] = got
+        send_z(t)
+
+    def z_arrive(t, half):
+        ref = zr.at[t, pl.ds(0, NZ // 2 - half)]
+        pltpu.make_async_copy(ref, ref, z_recv.at[t, half]).wait()
+
+    def pair_at(o):
+        return (z // 2 + PAIR_ORDER[o]) % (NZ // 2)
+
+    def spread(t, half):
+        for o in range(4 * half, 4 * half + 4):
+            rows = zr[t, pl.ds(2 * pair_at(o), 2)].reshape(2 * ZSLOT, LANES)
+            got = mm(p2[o], rows).astype(BF16).reshape(NPB, 8, LANES)
+            pe[t, :, 8 * o : 8 * o + 8, :] = got
+        rows = pl.ds(32 * half, 32)
         for dy, dx in P_ORDER:
             there = ((y + dy) % NY) * NX + (x + dx) % NX
-            remote(pe.at[t, there], pr.at[t, pb], p_send.at[t], p_recv.at[t], dev(dy=dy, dx=dx))
-        pr[t, pb] = pe[t, pb]
+            remote(
+                pe.at[t, there, rows], pr.at[t, pb, rows],
+                p_send.at[t, half], p_recv.at[t, half], dev(dy=dy, dx=dx),
+            )
+        pr[t, pb, rows] = pe[t, pb, rows]
 
     def p_arrive(t):
-        ref = pr.at[t, pl.ds(0, NPB - 1)]
-        pltpu.make_async_copy(ref, ref, p_recv.at[t]).wait()
-
-    def multiply(g):
-        score[...] = jnp.zeros_like(score)
+        for half in (0, 1):
+            ref = pr.at[t, pl.ds(0, NPB - 1), pl.ds(0, 32)]
+            pltpu.make_async_copy(ref, ref, p_recv.at[t, half]).wait()
+
+    def multiply(g, start, size, first=False):
+        if first:
+            score[...] = jnp.zeros_like(score)
 
         def some(i, carry):
-            k = pl.ds(pl.multiple_of(i * KSTEP, KSTEP), KSTEP)
+            k = pl.ds(pl.multiple_of(start + i * KSTEP, KSTEP), KSTEP)
             held = q_all[g, :, :, k].reshape(LANES, KSTEP)
             for s in (0, 1):
                 score[s] += mm(a_all[s, :, k], held, ((1,), (1,)))
             return carry
 
-        lax.fori_loop(0, K // KSTEP, some, 0)
+        lax.fori_loop(0, size // KSTEP, some, 0)
+
+    def weigh(g):
         pack(g, *[(score[s] * rescol[s]).astype(BF16) for s in (0, 1)])
 
     def finish(g):
@@ -248,11 +272,11 @@
     def meta_plane():
         ref = zmr.at[pl.ds(0, NZ - 1)]
         pltpu.make_async_copy(ref, ref, meta_recv.at[0]).wait()
-        for pair in range(NZ // 2):
-            both = zmr[2 * pair].astype(F32) + zmr[2 * pair + 1].astype(F32)
+        for o in range(NZ // 2):
+            both = zmr[2 * pair_at(o)].astype(F32) + zmr[2 * pair_at(o) + 1].astype(F32)
             both = both[:, 0 : 2 * ZSLOT]
-            p2[pair] = onehot(iota((128, 2 * ZSLOT), 0) == both[1:2].astype(I32) - 1)
-            pmf[pair : pair + 1] = mm(both.astype(BF16), p2[pair], ((1,), (1,)))[2:3]
+            p2[o] = onehot(iota((128, 2 * ZSLOT), 0) == both[1:2].astype(I32) - 1)
+            pmf[o : o + 1] = mm(both.astype(BF16), p2[o], ((1,), (1,)))[2:3]
         pms[...] = pmf[...].astype(BF16)
         for dy, dx in P_ORDER:
             remote(pms, pmr.at[pb], meta_send.at[1], meta_recv.at[1], dev(dy=dy, dx=dx))
@@ -269,51 +293,61 @@
         hit = value.astype(I32) - 1 == iota((NPB * PSLOT, 128), 1)
         smat[...] = jnp.where(hit, 1.0, 0.0).T.astype(BF16)
 
-    z_tell()
     step_f(0)
     step_s(0)
+    z_tell()
     step_f(1)
     pair_a = remote(train, a_all.at[c], d_send.at[1], d_recv.at[1], dev(dc=1))
-    pair_bundle.wait()
-    prepare()
-    z_hear(range(0, 3))
+    meta_own()
+    pair_bundle = remote(bundle.at[c], bundle.at[c], d_send.at[0], d_recv.at[0], dev(dc=1))
     step_b(0)
     for df in (1, 2, 3):
         for path in (0, 1):
             z_share(path, df, 0)
     step_s(1)
+    step_f(2)
+    pair_bundle.wait()
+    prepare()
+    z_hear()
+    meta_z()
     for path in (0, 1):
         arrive(0, path, 1, 3)
     for ds in (1, 2, 3):
         for path in (0, 1):
             z_share(path, 0, ds)
-    z_hear(range(3, NZ // 2))
-    meta_z()
-    step_b(1)
     for path in (0, 1):
         arrive(0, path, 2, 9)
     for df in (1, 2, 3):
         for ds in (1, 2, 3):
             for path in (0, 1):
                 z_share(path, df, ds)
-    step_f(2)
+    step_b(1)
     step_s(2)
-    meta_plane()
     copy_a.wait()
     pair_a.wait()
+    own_half = (z % 2) * HALF_K
+    multiply(0, own_half, HALF_K, True)
+    meta_plane()
     z_shared()
-    multiply(0)
+    multiply(0, HALF_K - own_half, HALF_K)
+    weigh(0)
     step_b(2)
     step_g(1)
-    multiply(1)
+    multiply(1, 0, K, True)
+    weigh(1)
     meta_sum()
-    z_arrive(0)
-    spread(0)
-    step_g(2)
-    multiply(2)
+    for half in (0, 1):
+        z_arrive(0, half)
+        spread(0, half)
+    for part in (0, 1):
+        step_g(2, part)
+        for path in (0, 1):
+            multiply(2, path * HALF_K + part * QUARTER_K, QUARTER_K, part + path == 0)
+    weigh(2)
     pair_acc = [finish(0)]
-    z_arrive(1)
-    spread(1)
+    for half in (0, 1):
+        z_arrive(1, half)
+        spread(1, half)
     pair_acc.append(finish(1))
     total = place_columns(0, accb[0, c], c) + place_columns(1, accb[1, c], c)
     pair_acc[0].wait_recv()
@@ -321,8 +355,9 @@
     pair_acc[1].wait_recv()
     total += place_columns(1, resb[1], 1 - c)
     out[...] = total
-    z_arrive(2)
-    spread(2)
+    for half in (0, 1):
+        z_arrive(2, half)
+        spread(2, half)
     pair_acc.append(finish(2))
     total = out[...] + place_columns(2, accb[2, c], c)
     pair_acc[2].wait_recv()
@@ -332,12 +367,14 @@
         cp.wait_send()
     for g in range(GROUPS):
         for path in (0, 1):
-            ref = q_all.at[g, pl.ds(0, 15), :, pl.ds(0, HALF_K if g > 0 else QUARTER_K)]
-            pltpu.make_async_copy(ref, ref, ag_send.at[g, path]).wait()
+            for part in parts(g):
+                ref = q_all.at[g, pl.ds(0, 15), :, pl.ds(0, HALF_K if g == 1 else QUARTER_K)]
+                pltpu.make_async_copy(ref, ref, ag_send.at[g, path, part]).wait()
         ref = zs.at[g, pl.ds(0, NZ - 1)]
         pltpu.make_async_copy(ref, ref, z_send.at[g]).wait()
-        ref = pe.at[g, pl.ds(0, NPB - 1)]
-        pltpu.make_async_copy(ref, ref, p_send.at[g]).wait()
+        for half in (0, 1):
+            ref = pe.at[g, pl.ds(0, NPB - 1), pl.ds(0, 32)]
+            pltpu.make_async_copy(ref, ref, p_send.at[g, half]).wait()
     ref = q_all.at[0, pl.ds(0, NPB - 1), :, pl.ds(0, HALF_K)]
     pltpu.make_async_copy(ref, ref, zq_send).wait()
     ref = zms.at[pl.ds(0, NZ - 1)]
@@ -380,21 +417,21 @@
             pltpu.SemaphoreType.REGULAR,
             pltpu.SemaphoreType.REGULAR,
             dma((5,)),
-            dma((GROUPS, 2, 3)),
-            dma((GROUPS, 2)),
+            dma((GROUPS, 2, 3, 2)),
+            dma((GROUPS, 2, 2)),
             dma,
             dma,
             dma((2,)),
             dma((2,)),
+            dma((t, 2)),
             dma((t,)),
-            dma((t,)),
-            dma((t,)),
-            dma((t,)),
+            dma((t, 2)),
+            dma((t, 2)),
             dma((2 + GROUPS,)),
             dma((2 + GROUPS,)),
         ],
         compiler_params=pltpu.CompilerParams(
-            collective_id=1, has_side_effects=True, vmem_limit_bytes=48 * 1024 * 1024
+            collective_id=1, has_side_effects=True
         ),
         name="scores",
     )(

time: 80.8 us -> 76.4 us (0.946)
  local copies, waits for them, and re-layouts: 5.96 us -> 1.62 us
    unnamed x11 -> x1, local copies, waits for them, and re-layouts: 5.96 us -> 1.62 us
where the time goes in v3:
time: 76.4 us; the launch traced here: 76.3 us
  Pallas kernels  74.6 us (98%)
  local copies, waits for them, and re-layouts  1.62 us (2%)
    pallas_call x1, Pallas kernels, on_device(): pl.pallas_call(kernel, out_shape=jax.ShapeDtypeStruct((SHARE, QUERIES), F...  74.6 us
    unnamed x1, local copies, waits for them, and re-layouts  1.62 us

profile of v3, /device:TPU:1, one launch (start us, length us, event | category | flops | bytes accessed | tf_op | source)
XLA Modules:
  0.0 76.3 jit_solution(9716851646075777891)
XLA Ops:
  0.0 74.6 %scores.1 = f32[64,768]{1,0:T(8,128)} custom-call(bf16[192,8192]{1,0:T(8,128)(2,1)} %train.1, bf16[48,8192]{1,0:T(8,128)(2,1)} %query.1, f32[1,192]{1,0:T(1,128)} %bitcast.4, s32[1,192]{1,0:T(1,128)} %bitcast.5, s32[256,128]{1,0:T(8,128)} %bitcast.3), custom_call_target="tpu_custom_call" | custom-call | tf_op jit(solution)/shard_map/scores/pallas_call | solution.py:391
  74.7 1.6 %copy.7 = f32[64,768]{1,0:T(8,128)} copy(f32[64,768]{1,0:T(8,128)} %scores.1) | data formatting | bytes 393216
